TPU v7x, 128 devices: a whole 4x4x4 slice. The times are simulated.
128 devices in a mesh: ctx: 8 (over y_lo, x), tp: 16 (over z, y_hi, core).
Axes of the slice: x: 4, y: 4 (y_hi: 2, y_lo: 2; y = y_hi * 2 + y_lo), z: 4, core: 2. Of those that a mesh axis runs over, the one named last changes fastest.
Arguments:
- inputs: bfloat16 [6144, 4096], P('ctx', 'tp'), may hold values from -6 to 6
- in_proj: bfloat16 [4096, 3, 4096], P(None, None, 'tp'), may hold values from -0.125 to 0.125
- out_proj: bfloat16 [4096, 4096], P('tp'), may hold values from -0.125 to 0.125
- short_taps: float32 [7, 3, 4096], P(None, None, 'tp'), may hold values from -2.4 to 2.4
- skip_gain: float32 [4096], P('tp'), may hold values from -4 to 4
- long_taps: bfloat16 [128, 256], P(None, 'tp'), may hold values from -1 to 1
- cotangent: bfloat16 [6144, 4096], P('ctx', 'tp'), may hold values from -1.5 to 1.5
Outputs:
- layer_out: bfloat16 [6144, 4096], P('ctx', 'tp')
- grad_inputs: bfloat16 [6144, 4096], P('ctx', 'tp')
- grad_in_proj: float32 [4096, 3, 4096], P('ctx', None, 'tp')
- grad_out_proj: float32 [4096, 4096], P('tp', 'ctx')
- grad_long_taps: float32 [128, 256], P(None, 'tp')
All inputs are finite; a program needn't handle non-finite values.
Results may differ from a plain program's by a relative error of at most 0.014.
Values may be sent and summed in bfloat16 or wider, within the bound.
A program may use at most 128 MiB of HBM per device.

v0:
```python
import jax
import jax.numpy as jnp
from jax import lax
from jax.sharding import PartitionSpec as P

GROUP = 16
LTAPS = 128
STAPS = 7


def shifted(shard, axis, by):
    peers = lax.axis_size(axis)
    pairs = [(i, i + by) for i in range(peers) if 0 <= i + by < peers]
    return lax.ppermute(shard, axis, pairs)


def tap_sum(padded, tap_table, row_count, causal):
    tap_count = tap_table.shape[0]
    running = jnp.zeros((row_count,) + padded.shape[1:], jnp.float32)
    for lag_index in range(tap_count):
        offset = tap_count - 1 - lag_index if causal else lag_index
        running = running + tap_table[lag_index] * padded[offset : offset + row_count].astype(
            jnp.float32
        )
    return running


def make_bands(tap_table):
    tap_count = tap_table.shape[0]
    row_ids = lax.broadcasted_iota(jnp.int32, (tap_count, tap_count, tap_count), 0)
    col_ids = lax.broadcasted_iota(jnp.int32, (tap_count, tap_count, tap_count), 1)
    tap_ids = lax.broadcasted_iota(jnp.int32, (tap_count, tap_count, tap_count), 2)
    lag_ids = row_ids - col_ids
    lower_hot = (lag_ids == tap_ids).astype(jnp.bfloat16)
    upper_hot = (lag_ids + tap_count == tap_ids).astype(jnp.bfloat16)
    lower_band = jnp.einsum(
        "abj,jg->gab", lower_hot, tap_table, preferred_element_type=jnp.float32
    ).astype(jnp.bfloat16)
    upper_band = jnp.einsum(
        "abj,jg->gab", upper_hot, tap_table, preferred_element_type=jnp.float32
    ).astype(jnp.bfloat16)
    return (lower_band, upper_band)


def lag_totals(matrix):
    group_count = matrix.shape[0]
    tap_count = matrix.shape[1]
    flipped = matrix[:, :, ::-1]
    padded = jnp.pad(flipped, ((0, 0), (0, 0), (0, tap_count)))
    flat_rows = padded.reshape(group_count, 2 * tap_count * tap_count)[
        :, : tap_count * (2 * tap_count - 1)
    ]
    return flat_rows.reshape(group_count, tap_count, 2 * tap_count - 1).sum(axis=1)


def local(inputs, in_proj, out_proj, short_taps, skip_gain, long_taps, cotangent):
    token_count = inputs.shape[0]
    model_width = in_proj.shape[0]
    channels_dev = in_proj.shape[2]
    groups_dev = long_taps.shape[1]
    tile_count = token_count // LTAPS
    in_matrix = in_proj.reshape(model_width, 3 * channels_dev)
    inputs_full = lax.all_gather(inputs, "tp", axis=1, tiled=True)
    projected = jnp.dot(inputs_full, in_matrix, preferred_element_type=jnp.float32).astype(
        jnp.bfloat16
    )
    projected = projected.reshape(token_count, 3, channels_dev)
    short_prev = shifted(projected[token_count - STAPS + 1 :], "ctx", 1)
    mixed = tap_sum(jnp.concatenate([short_prev, projected], axis=0), short_taps, token_count, True)
    query, keyed, valued = (mixed[:, 0], mixed[:, 1], mixed[:, 2])
    gated = (keyed * valued).astype(jnp.bfloat16)
    long_prev = shifted(gated[token_count - LTAPS + 1 :], "ctx", 1)
    lower_band, upper_band = make_bands(long_taps)
    gated_tiles = jnp.concatenate(
        [jnp.zeros((1, channels_dev), jnp.bfloat16), long_prev, gated], axis=0
    )
    gated_tiles = gated_tiles.reshape(tile_count + 1, LTAPS, groups_dev, GROUP)
    gated_now = gated_tiles[1:]
    gated_before = gated_tiles[:-1]
    conv_part = jnp.einsum(
        "gab,nbgc->nagc", lower_band, gated_now, preferred_element_type=jnp.float32
    )
    conv_part = conv_part + jnp.einsum(
        "gab,nbgc->nagc", upper_band, gated_before, preferred_element_type=jnp.float32
    )
    wave = conv_part.reshape(token_count, channels_dev) + skip_gain * gated.astype(jnp.float32)
    filtered = (query * wave).astype(jnp.bfloat16)
    out_terms = jnp.dot(filtered, out_proj, preferred_element_type=jnp.float32)
    layer_out = lax.psum_scatter(
        out_terms.astype(jnp.bfloat16), "tp", scatter_dimension=1, tiled=True
    )
    cot_full = lax.all_gather(cotangent, "tp", axis=1, tiled=True)
    grad_filtered = lax.dot_general(
        cot_full, out_proj, (((1,), (1,)), ((), ())), preferred_element_type=jnp.float32
    )
    out_grad_terms = lax.dot_general(
        filtered, cot_full, (((0,), (0,)), ((), ())), preferred_element_type=jnp.float32
    )
    grad_out_proj = lax.psum_scatter(
        out_grad_terms.astype(jnp.bfloat16), "ctx", scatter_dimension=1, tiled=True
    ).astype(jnp.float32)
    grad_wave = (grad_filtered * query).astype(jnp.bfloat16)
    grad_query = grad_filtered * wave
    wave_next = shifted(grad_wave[: LTAPS - 1], "ctx", -1)
    wave_tiles = jnp.concatenate(
        [grad_wave, wave_next, jnp.zeros((1, channels_dev), jnp.bfloat16)], axis=0
    )
    wave_tiles = wave_tiles.reshape(tile_count + 1, LTAPS, groups_dev, GROUP)
    wave_now = wave_tiles[:-1]
    wave_after = wave_tiles[1:]
    back_part = jnp.einsum(
        "gab,nagc->nbgc", lower_band, wave_now, preferred_element_type=jnp.float32
    )
    back_part = back_part + jnp.einsum(
        "gab,nagc->nbgc", upper_band, wave_after, preferred_element_type=jnp.float32
    )
    grad_gated = back_part.reshape(token_count, channels_dev) + skip_gain * grad_wave.astype(
        jnp.float32
    )
    lower_corr = jnp.einsum(
        "nagc,nbgc->gab", wave_now, gated_now, preferred_element_type=jnp.float32
    )
    upper_corr = jnp.einsum(
        "nagc,nbgc->gab", wave_now, gated_before, preferred_element_type=jnp.float32
    )
    lower_sums = lag_totals(lower_corr)
    upper_sums = lag_totals(upper_corr)
    tap_grads = lower_sums[:, LTAPS - 1 :] + jnp.pad(upper_sums[:, : LTAPS - 1], ((0, 0), (1, 0)))
    grad_long_taps = lax.psum(tap_grads.T, "ctx")
    grad_mixed = jnp.stack([grad_query, grad_gated * valued, grad_gated * keyed], axis=1).astype(
        jnp.bfloat16
    )
    mixed_next = shifted(grad_mixed[: STAPS - 1], "ctx", -1)
    grad_projected = tap_sum(
        jnp.concatenate([grad_mixed, mixed_next], axis=0), short_taps, token_count, False
    )
    grad_matrix = grad_projected.astype(jnp.bfloat16).reshape(token_count, 3 * channels_dev)
    input_terms = lax.dot_general(
        grad_matrix, in_matrix, (((1,), (1,)), ((), ())), preferred_element_type=jnp.float32
    )
    grad_inputs = lax.psum_scatter(
        input_terms.astype(jnp.bfloat16), "tp", scatter_dimension=1, tiled=True
    )
    weight_grad = lax.psum_scatter(
        lax.dot_general(
            inputs_full, grad_matrix, (((0,), (0,)), ((), ())), preferred_element_type=jnp.float32
        ).astype(jnp.bfloat16),
        "ctx",
        scatter_dimension=0,
        tiled=True,
    ).astype(jnp.float32)
    grad_in_proj = weight_grad.reshape(weight_grad.shape[0], 3, channels_dev)
    return (layer_out, grad_inputs, grad_in_proj, grad_out_proj, grad_long_taps)


def solution(mesh):
    placed = (
        P("ctx", "tp"),
        P(None, None, "tp"),
        P("tp", None),
        P(None, None, "tp"),
        P("tp"),
        P(None, "tp"),
        P("ctx", "tp"),
    )
    return jax.shard_map(
        local,
        mesh=mesh,
        in_specs=placed,
        out_specs=(
            P("ctx", "tp"),
            P("ctx", "tp"),
            P("ctx", None, "tp"),
            P("tp", "ctx"),
            P(None, "tp"),
        ),
        check_vma=False,
    )
```

profile of v0, /device:TPU:0, one launch (start us, length us, event | category | flops | bytes accessed | tf_op | source)
XLA Modules:
  0.0 505.0 jit_solution(2170695225887025520)
XLA Ops:
  8.7 8.7 %copy.27 = bf16[4096,3,256]{0,2,1:T(8,128)(2,1)} copy(bf16[4096,3,256]{2,0,1:T(8,128)(2,1)} %param.8) | data formatting | bytes 12582912 | tf_op args[1]
  17.5 2.2 fusion.9
  19.7 60.1 %all-gather.3.cloned.1.call-done = bf16[768,4096]{1,0:T(8,128)(2,1)} async-done(((bf16[768,256]{1,0:T(8,128)(2,1)}), bf16[768,4096]{1,0:T(8,128)(2,1)}) %all-gather.3.cloned.1.call-update) | async-done | bytes 6291472 | tf_op jit(solution)/shard_map/all_gather | solution.py:63
  79.8 9.0 %convolution_convert_fusion.3 = bf16[768,768]{1,0:T(8,128)(2,1)S(1)} fusion(bf16[768,4096]{1,0:T(8,128)(2,1)} %all-gather.3.cloned.1.call-done, bf16[4096,768]{0,1:T(8,128)(2,1)} %bitcast.122), kind=kOutput, calls=%fused_computation.18 | convolution fusion | flops 4832428032 | bytes 13762560 | tf_op jit(solution)/shard_map/dot_general | solution.py:64
  88.8 3.4 collective-permute-start
  92.2 2.5 fusion.8
  94.8 1.4 copy.28
  96.2 1.6 copy.29
  97.8 2.1 multiply_add_fusion
  100.0 1.4 copy-done.1
  102.2 44.4 %all-gather.5.cloned.1.call-done = bf16[768,4096]{1,0:T(8,128)(2,1)} async-done(((bf16[768,256]{1,0:T(8,128)(2,1)}), bf16[768,4096]{1,0:T(8,128)(2,1)}) %all-gather.5.cloned.1.call-update) | async-done | bytes 6291472 | tf_op jit(solution)/shard_map/all_gather | solution.py:92
  146.6 6.2 %multiply_convert_fusion = (bf16[768,256]{1,0:T(8,128)(2,1)S(1)}, bf16[768,256]{1,0:T(8,128)(2,1)S(1)}, f32[768,256]{1,0:T(8,128)}) fusion(f32[768,3,256]{2,0,1:T(8,128)} %copy-done.1, bf16[768,4096]{1,0:T(8,128)(2,1)} %all-gather.5.cloned.1.call-done, bf16[256,4096]{1,0:T(8,128)(2,1)S(1)} %copy-done), kind=kOutput, calls=%fused_computation.50 | convolution fusion | flops 1611399168 | bytes 12320768 | tf_op jit(solution)/shard_map/dot_general | solution.py:93
  154.3 1.9 copy.32
  156.2 2.3 convert_element_type.117
  160.4 4.7 collective-permute-start.1
  165.1 2.2 slice.139
  167.4 2.4 fusion.22
  169.8 1.5 fusion.20
  171.3 1.9 pad_maximum_fusion.3
  175.7 1.5 fusion.5
  178.8 1.9 copy.35
  180.7 1.4 slice.138
  182.2 1.8 fusion.6
  185.6 3.0 fusion.26
  189.3 5.9 %convolution_convert_fusion.2 = bf16[256,4096]{1,0:T(8,128)(2,1)} fusion(bf16[768,256]{1,0:T(8,128)(2,1)S(1)} %get-tuple-element.17, bf16[768,4096]{1,0:T(8,128)(2,1)} %all-gather.5.cloned.1.call-done), kind=kOutput, calls=%fused_computation.9 | convolution fusion | flops 1611661312 | bytes 8781824 | tf_op jit(solution)/shard_map/dot_general | solution.py:96
  195.5 1.3 collective-permute-start.3
  196.8 4.3 collective-permute-done.3
  201.2 3.0 add_convert_fusion
  204.2 1.6 copy.48
  205.7 9.7 %fusion.2 = bf16[4096,768]{0,1:T(8,128)(2,1)} fusion(bf16[768,768]{0,1:T(8,128)(2,1)S(1)} %bitcast.128, bf16[768,4096]{1,0:T(8,128)(2,1)} %all-gather.3.cloned.1.call-done), kind=kOutput, calls=%fused_computation.8 | convolution fusion | flops 4834983936 | bytes 13762560 | tf_op jit(solution)/shard_map/dot_general | solution.py:145
  216.5 4.4 convolution_convert_fusion
  222.2 9.7 %bitcast_convert_fusion = bf16[768,4096]{1,0:T(8,128)(2,1)} fusion(bf16[768,3,256]{2,0,1:T(8,128)(2,1)S(1)} %copy-done.4, bf16[4096,3,256]{2,0,1:T(8,128)(2,1)} %param.8), kind=kOutput, calls=%fused_computation | convolution fusion | flops 4834983936 | bytes 13762560 | tf_op jit(solution)/shard_map/dot_general | solution.py:138
  233.1 1.3 convolution_bitcast_fusion.1
  234.4 7.5 %rev.6 = f32[16,128,128]{2,1,0:T(8,128)S(1)} reverse(f32[16,128,128]{2,1,0:T(8,128)} %convolution_bitcast_fusion.1), dimensions={2} | reverse | bytes 2097152 | tf_op jit(solution)/shard_map/rev | solution.py:48
  243.4 1.5 slice.177
  244.9 6.4 %reshape.63 = f32[16,128,255]{2,1,0:T(8,128)} reshape(f32[16,32640]{1,0:T(8,128)} %slice.177) | data formatting | bytes 4177920 | tf_op jit(solution)/shard_map/reshape | solution.py:53
  251.3 1.8 reduce_sum.18
  253.1 1.3 convolution_bitcast_fusion
  254.4 7.5 %rev.7 = f32[16,128,128]{2,1,0:T(8,128)S(1)} reverse(f32[16,128,128]{2,1,0:T(8,128)} %convolution_bitcast_fusion), dimensions={2} | reverse | bytes 2097152 | tf_op jit(solution)/shard_map/rev | solution.py:48
  263.4 1.5 slice.179
  264.9 6.2 %reshape.65 = f32[16,128,255]{2,1,0:T(8,128)} reshape(f32[16,32640]{1,0:T(8,128)} %slice.179) | data formatting | bytes 4177920 | tf_op jit(solution)/shard_map/reshape | solution.py:53
  271.1 1.8 reduce_sum.19
  272.9 22.4 %psum.7 = f32[128,16]{0,1:T(8,128)} all-reduce(f32[128,16]{0,1:T(8,128)S(1)} %fusion.35), channel_id=1, replica_groups=mesh['ctx'=8,'tp'=16] {'ctx'}, use_global_device_ids=true, to_apply=%region_6.7 | all-reduce | flops 2048 | bytes 16384 | tf_op jit(solution)/shard_map/psum | solution.py:129
  295.3 1.8 convert_element_type.140
  297.1 14.2 %reduce-scatter.9.cloned.1.call-done = bf16[512,768]{0,1:T(8,128)(2,1)} async-done(((bf16[4096,768]{0,1:T(8,128)(2,1)}), bf16[512,768]{0,1:T(8,128)(2,1)}) %reduce-scatter.9.cloned.1.call-update) | async-done | bytes 786448 | tf_op jit(solution)/shard_map/reduce_scatter | solution.py:144
  311.3 2.5 copy.53
  313.9 90.6 %reduce-scatter.5.cloned.1.call-done = bf16[768,256]{1,0:T(8,128)(2,1)} async-done(((bf16[768,4096]{1,0:T(8,128)(2,1)}), bf16[768,256]{1,0:T(8,128)(2,1)}) %reduce-scatter.5.cloned.1.call-update) | async-done | bytes 393232 | tf_op jit(solution)/shard_map/reduce_scatter | solution.py:89
  404.5 93.7 %reduce-scatter.7.cloned.1.call-done = bf16[768,256]{1,0:T(8,128)(2,1)} async-done(((bf16[768,4096]{1,0:T(8,128)(2,1)}), bf16[768,256]{1,0:T(8,128)(2,1)}) %reduce-scatter.7.cloned.1.call-update) | async-done | bytes 393232 | tf_op jit(solution)/shard_map/reduce_scatter | solution.py:141
  (90 shorter events, 18.9 us)
Async XLA Ops:
  7.2 139.4 %copy-start = (bf16[256,4096]{1,0:T(8,128)(2,1)S(1)}, bf16[256,4096]{1,0:T(8,128)(2,1)}, u32[]{:S(2)}) copy-start(bf16[256,4096]{1,0:T(8,128)(2,1)} %param.9) | copy-start | bytes 6291460
  7.2 72.6 %all-gather.3.cloned.1.call-start = ((), (), s32[]{:S(2)}) async-start(), calls=%async_computation.4 | async-start | bytes 6684672 | tf_op jit(solution)/shard_map/all_gather | solution.py:63
  7.9 138.7 %all-gather.5.cloned.1.call-start = ((), (), s32[]{:S(2)}) async-start(), calls=%async_computation.6 | async-start | bytes 6684672 | tf_op jit(solution)/shard_map/all_gather | solution.py:92
  8.7 8.8 %copy-start.20 = (f32[7,3,256]{2,0,1:T(8,128)S(1)}, f32[7,3,256]{2,0,1:T(8,128)}, u32[]{:S(2)}) copy-start(f32[7,3,256]{2,0,1:T(8,128)} %param.10) | copy-start | bytes 64516
  8.7 8.8 %copy-start.22 = (bf16[128,16]{0,1:T(8,128)(2,1)S(1)}, bf16[128,16]{0,1:T(8,128)(2,1)}, u32[]{:S(2)}) copy-start(bf16[128,16]{0,1:T(8,128)(2,1)} %param.12) | copy-start | bytes 12292
  8.7 286.6 %reduce-scatter.11.cloned.1.call-start = ((), (), s32[]{:S(2)}) async-start(), calls=%async_computation.9 | async-start | bytes 2359296 | tf_op jit(solution)/shard_map/reduce_scatter | solution.py:99
  17.5 80.3 %copy-start.14 = (f32[3,256]{1,0:T(4,128)}, f32[3,256]{1,0:T(4,128)S(1)}, u32[]{:S(2)}) copy-start(f32[3,256]{1,0:T(4,128)S(1)} %get-tuple-element.31) | copy-start | bytes 9220
  17.5 80.3 %copy-start.16 = (f32[3,256]{1,0:T(4,128)}, f32[3,256]{1,0:T(4,128)S(1)}, u32[]{:S(2)}) copy-start(f32[3,256]{1,0:T(4,128)S(1)} %get-tuple-element.32) | copy-start | bytes 9220
  88.8 8.9 %collective-permute-start = (bf16[6,3,256]{2,0,1:T(8,128)(2,1)S(1)}, bf16[6,3,256]{2,0,1:T(8,128)(2,1)S(1)}, u32[]{:S(2)}, u32[]{:S(2)}) collective-permute-start(bf16[6,3,256]{2,0,1:T(8,128)(2,1)S(1)} %bitcast.132), channel_id=1, source_target_pairs={{0,16},{16,32},{32,48},{48,64},{64,80},{80,96},{96,112},{1,17},{17... | collective-permute-start | bytes 27656 | tf_op jit(solution)/shard_map/ppermute | solution.py:14
  94.8 3.0 copy-start.18
  100.0 1.4 copy-start.1
  152.8 14.6 %copy-start.8 = (bf16[768,256]{1,0:T(8,128)(2,1)}, bf16[768,256]{1,0:T(8,128)(2,1)S(1)}, u32[]{:S(2)}) copy-start(bf16[768,256]{1,0:T(8,128)(2,1)S(1)} %get-tuple-element.19) | copy-start | bytes 1179652
  152.8 18.6 %copy-start.5 = (bf16[768,256]{1,0:T(8,128)(2,1)}, bf16[768,256]{1,0:T(8,128)(2,1)S(1)}, u32[]{:S(2)}) copy-start(bf16[768,256]{1,0:T(8,128)(2,1)S(1)} %get-tuple-element.18) | copy-start | bytes 1179652
  152.8 14.6 %copy-start.7 = (bf16[16,128,128,1]{2,0,1,3:T(8,128)(2,1)S(1)}, bf16[16,128,128,1]{2,0,1,3:T(8,128)(2,1)}, u32[]{:S(2)}) copy-start(bf16[16,128,128,1]{2,0,1,3:T(8,128)(2,1)} %fusion.8) | copy-start | bytes 1572868
  159.1 12.2 %collective-permute-start.2 = (bf16[127,256]{1,0:T(8,128)(2,1)}, bf16[127,256]{1,0:T(8,128)(2,1)S(1)}, u32[]{:S(2)}, u32[]{:S(2)}) collective-permute-start(bf16[127,256]{1,0:T(8,128)(2,1)} %slice.169), channel_id=1, source_target_pairs={{16,0},{32,16},{48,32},{64,48},{80,64},{96,80},{112,96},{17,1},{33... | collective-permute-start | bytes 195080 | tf_op jit(solution)/shard_map/ppermute | solution.py:14
  160.4 10.9 %collective-permute-start.1 = (bf16[127,256]{1,0:T(8,128)(2,1)}, bf16[127,256]{1,0:T(8,128)(2,1)S(1)}, u32[]{:S(2)}, u32[]{:S(2)}) collective-permute-start(bf16[127,256]{1,0:T(8,128)(2,1)} %slice.168), channel_id=1, source_target_pairs={{0,16},{16,32},{32,48},{48,64},{64,80},{80,96},{96,112},{1,17},{17... | collective-permute-start | bytes 195080 | tf_op jit(solution)/shard_map/ppermute | solution.py:14
  177.4 4.7 copy-start.6
  182.1 2.1 copy-start.9
  184.0 1.6 copy-start.21
  188.5 0.7 copy-start.2
  195.2 116.1 %reduce-scatter.9.cloned.1.call-start = ((), (), s32[]{:S(2)}) async-start(), calls=%async_computation.8 | async-start | bytes 7077888 | tf_op jit(solution)/shard_map/reduce_scatter | solution.py:144
  195.3 5.9 %copy-start.15 = (f32[3,256]{1,0:T(4,128)S(1)}, f32[3,256]{1,0:T(4,128)}, u32[]{:S(2)}) copy-start(f32[3,256]{1,0:T(4,128)} %copy-done.14) | copy-start | bytes 9220
  195.3 5.9 %copy-start.17 = (f32[3,256]{1,0:T(4,128)S(1)}, f32[3,256]{1,0:T(4,128)}, u32[]{:S(2)}) copy-start(f32[3,256]{1,0:T(4,128)} %copy-done.16) | copy-start | bytes 9220
  195.3 5.9 %copy-start.19 = (f32[1,3,256]{2,1,0:T(4,128)S(1)}, f32[1,3,256]{2,1,0:T(4,128)}, u32[]{:S(2)}) copy-start(f32[1,3,256]{2,1,0:T(4,128)} %copy-done.18) | copy-start | bytes 9220
  195.5 5.6 %collective-permute-start.3 = (bf16[6,3,256]{2,0,1:T(8,128)(2,1)S(1)}, bf16[6,3,256]{2,0,1:T(8,128)(2,1)S(1)}, u32[]{:S(2)}, u32[]{:S(2)}) collective-permute-start(bf16[6,3,256]{2,0,1:T(8,128)(2,1)S(1)} %slice.170), channel_id=1, source_target_pairs={{16,0},{32,16},{48,32},{64,48},{80,64},{96,80},{112,96},{17,1},{33... | collective-permute-start | bytes 27656 | tf_op jit(solution)/shard_map/ppermute | solution.py:14
  215.5 1.0 copy-start.3
  215.5 189.0 %reduce-scatter.5.cloned.1.call-start = ((), (), s32[]{:S(2)}) async-start(), calls=%async_computation.5 | async-start | bytes 6684672 | tf_op jit(solution)/shard_map/reduce_scatter | solution.py:89
  220.9 1.3 copy-start.4
  220.9 277.3 %reduce-scatter.7.cloned.1.call-start = ((), (), s32[]{:S(2)}) async-start(), calls=%async_computation.7 | async-start | bytes 6684672 | tf_op jit(solution)/shard_map/reduce_scatter | solution.py:141
  231.9 1.0 copy-start.11
  231.9 1.2 copy-start.13
  244.9 8.1 %copy-start.10 = (bf16[6,128,16,16]{1,0,3,2:T(8,128)(2,1)S(1)}, bf16[6,128,16,16]{1,0,3,2:T(8,128)(2,1)}, u32[]{:S(2)}) copy-start(bf16[6,128,16,16]{1,0,3,2:T(8,128)(2,1)} %copy-done.9) | copy-start | bytes 1179652
  244.9 8.1 %copy-start.12 = (bf16[6,128,16,16]{1,0,3,2:T(8,128)(2,1)S(1)}, bf16[6,128,16,16]{1,0,3,2:T(8,128)(2,1)}, u32[]{:S(2)}) copy-start(bf16[6,128,16,16]{1,0,3,2:T(8,128)(2,1)} %slice.139) | copy-start | bytes 1179652
Sparse Core Ops, SparseCore 0:
  10.4 69.3 all-gather.2
  82.1 64.4 all-gather.4
  195.4 41.2 reduce-scatter.10
  239.0 72.3 reduce-scatter.8
  316.0 88.4 reduce-scatter.4
  409.7 88.4 reduce-scatter.6
where the time goes:
time: 507 us; the launch traced here: 505 us
  waiting for transfers between devices  309 us (61%)
  local copies, waits for them, and re-layouts  72.2 us (14%)
  matrix products  59.6 us (12%)
  blocking collectives  22.4 us (4%)
  other arithmetic  16.4 us (3%)
  between operations  14.6 us (3%)
  starting transfers between devices  11.1 us (2%)
    reduce_scatter x1, waiting for transfers between devices, local(): lax.psum_scatter(input_terms.astype(jnp.bfloat16), 'tp', scatter_dimensio...  93.7 us
    reduce_scatter x1, waiting for transfers between devices, local(): lax.psum_scatter(out_terms.astype(jnp.bfloat16), 'tp', scatter_dimension=...  90.6 us
    all_gather x1, waiting for transfers between devices, local(): inputs_full = lax.all_gather(inputs, 'tp', axis=1, tiled=True)  60.1 us
    all_gather x1, waiting for transfers between devices, local(): cot_full = lax.all_gather(cotangent, 'tp', axis=1, tiled=True)  44.4 us
    psum x1, blocking collectives, local(): grad_long_taps = lax.psum(tap_grads.T, 'ctx')  22.4 us
    unnamed x56, local copies, waits for them, and re-layouts  19.3 us
    rev x2, local copies, waits for them, and re-layouts, lag_totals(): flipped = matrix[:, :, ::-1]  15 us
    reduce_scatter x1, waiting for transfers between devices, local(): lax.psum_scatter(lax.dot_general(inputs_full, grad_matrix, (((0,), (0,)),...  14.2 us
  transfers between devices with their start and end apart: 10, of which 6 were waited for; matrix products, arithmetic and copies ran while one was open for 21% of the time, Pallas kernels for 0%

commit v1 on v0

--- a/solution.py
+++ b/solution.py
@@ -60,7 +60,9 @@
     groups_dev = long_taps.shape[1]
     tile_count = token_count // LTAPS
     in_matrix = in_proj.reshape(model_width, 3 * channels_dev)
-    inputs_full = lax.all_gather(inputs, "tp", axis=1, tiled=True)
+    inputs_full = jnp.concatenate(
+        lax.all_to_all(jnp.stack([inputs] * lax.axis_size("tp")), "tp", 0, 0), axis=1
+    )
     projected = jnp.dot(inputs_full, in_matrix, preferred_element_type=jnp.float32).astype(
         jnp.bfloat16
     )

time: 507 us -> 482 us (0.951)
  waiting for transfers between devices: 309 us -> 279 us
  starting transfers between devices: 11.1 us -> 19.3 us
    all_to_all x0 -> x1, waiting for transfers between devices: none -> 67.2 us  [local(): lax.all_to_all(jnp.stack([inputs] * lax.axis_size('tp')), 'tp', 0, 0)]
    all_gather x1 -> x0, waiting for transfers between devices: 60.1 us -> none  [local(): inputs_full = lax.all_gather(inputs, 'tp', axis=1, tiled=True)]
    all_gather x1, waiting for transfers between devices: 44.4 us -> 7.34 us  [local(): cot_full = lax.all_gather(cotangent, 'tp', axis=1, tiled=True)]
    all_to_all x0 -> x1, starting transfers between devices: none -> 8.18 us  [local(): lax.all_to_all(jnp.stack([inputs] * lax.axis_size('tp')), 'tp', 0, 0)]
    unnamed x56 -> x59, local copies, waits for them, and re-layouts: 19.3 us -> 21 us
  transfers between devices with their start and end apart: 10 -> 10, of which waited for: 6 -> 6; matrix products, arithmetic and copies ran while one was open for 21% -> 23% of each run, Pallas kernels for 0% -> 0%
where the time goes in v1:
time: 482 us; the launch traced here: 480 us
  waiting for transfers between devices  279 us (58%)
  local copies, waits for them, and re-layouts  70.5 us (15%)
  matrix products  58.9 us (12%)
  blocking collectives  22.2 us (5%)
  starting transfers between devices  19.3 us (4%)
  other arithmetic  15.7 us (3%)
  between operations  14.3 us (3%)
    reduce_scatter x1, waiting for transfers between devices, local(): lax.psum_scatter(input_terms.astype(jnp.bfloat16), 'tp', scatter_dimensio...  93.8 us
    reduce_scatter x1, waiting for transfers between devices, local(): lax.psum_scatter(out_terms.astype(jnp.bfloat16), 'tp', scatter_dimension=...  90.6 us
    all_to_all x1, waiting for transfers between devices, local(): lax.all_to_all(jnp.stack([inputs] * lax.axis_size('tp')), 'tp', 0, 0)  67.2 us
    psum x1, blocking collectives, local(): grad_long_taps = lax.psum(tap_grads.T, 'ctx')  22.2 us
    unnamed x59, local copies, waits for them, and re-layouts  21 us
    rev x2, local copies, waits for them, and re-layouts, lag_totals(): flipped = matrix[:, :, ::-1]  15 us
    reduce_scatter x1, waiting for transfers between devices, local(): lax.psum_scatter(lax.dot_general(inputs_full, grad_matrix, (((0,), (0,)),...  14.9 us
    reshape x2, local copies, waits for them, and re-layouts, lag_totals(): flat_rows.reshape(group_count, tap_count, 2 * tap_count - 1).sum(axis=1)  12.5 us
  transfers between devices with their start and end apart: 10, of which 6 were waited for; matrix products, arithmetic and copies ran while one was open for 23% of the time, Pallas kernels for 0%

profile of v1, /device:TPU:0, one launch (start us, length us, event | category | flops | bytes accessed | tf_op | source)
XLA Modules:
  0.0 479.9 jit_solution(611897426589506231)
XLA Ops:
  9.1 3.2 stack.14
  12.3 8.2 %all-to-all-start = ((bf16[16,768,256]{1,2,0:T(8,128)(2,1)}), bf16[16,768,256]{1,2,0:T(8,128)(2,1)}, u32[]{:S(2)}, u32[]{:S(2)}) async-start(bf16[16,768,256]{1,2,0:T(8,128)(2,1)} %stack.14), calls=%async_computation | async-start | bytes 12582912 | tf_op jit(solution)/shard_map/all_to_all | solution.py:64
  20.6 8.9 %copy.28 = bf16[4096,3,256]{0,2,1:T(8,128)(2,1)} copy(bf16[4096,3,256]{2,0,1:T(8,128)(2,1)} %param.8) | data formatting | bytes 12582912 | tf_op args[1]
  29.6 2.2 fusion.9
  31.8 67.2 %all-to-all-done = bf16[16,768,256]{1,2,0:T(8,128)(2,1)} async-done(((bf16[16,768,256]{1,2,0:T(8,128)(2,1)}), bf16[16,768,256]{1,2,0:T(8,128)(2,1)}, u32[]{:S(2)}, u32[]{:S(2)}) %all-to-all-start) | async-done | bytes 6291488 | tf_op jit(solution)/shard_map/all_to_all | solution.py:64
  99.0 9.3 %convolution_convert_fusion.3 = bf16[768,768]{1,0:T(8,128)(2,1)S(1)} fusion(bf16[768,4096]{0,1:T(8,128)(2,1)} %bitcast.1, bf16[4096,768]{0,1:T(8,128)(2,1)} %bitcast.125), kind=kOutput, calls=%fused_computation.18 | convolution fusion | flops 4832428032 | bytes 13762560 | tf_op jit(solution)/shard_map/dot_general | solution.py:66
  108.3 3.4 collective-permute-start
  111.8 2.5 fusion.8
  114.3 1.4 copy.29
  115.7 1.6 copy.30
  117.3 2.1 multiply_add_fusion
  119.5 1.4 copy-done.1
  121.9 1.4 fusion.22
  123.3 7.3 %all-gather.2.cloned.1.call-done = bf16[768,4096]{1,0:T(8,128)(2,1)} async-done(((bf16[768,256]{1,0:T(8,128)(2,1)}), bf16[768,4096]{1,0:T(8,128)(2,1)}) %all-gather.2.cloned.1.call-update) | async-done | bytes 6291472 | tf_op jit(solution)/shard_map/all_gather | solution.py:94
  130.7 6.2 %multiply_convert_fusion = (bf16[768,256]{1,0:T(8,128)(2,1)S(1)}, bf16[768,256]{1,0:T(8,128)(2,1)S(1)}, f32[768,256]{1,0:T(8,128)}) fusion(f32[768,3,256]{2,0,1:T(8,128)} %copy-done.1, bf16[768,4096]{1,0:T(8,128)(2,1)} %all-gather.2.cloned.1.call-done, bf16[256,4096]{1,0:T(8,128)(2,1)S(1)} %copy-done), kind=kOutput, calls=%fused_computation.50 | convolution fusion | flops 1611399168 | bytes 12320768 | tf_op jit(solution)/shard_map/dot_general | solution.py:95
  137.0 1.3 collective-permute-start.2
  138.3 4.7 collective-permute-start.1
  144.3 1.5 fusion.20
  145.9 1.9 pad_maximum_fusion.3
  150.2 1.5 fusion.5
  153.3 1.9 copy.36
  155.2 1.4 slice.138
  156.7 1.8 fusion.6
  160.1 3.0 fusion.26
  163.8 5.9 %convolution_convert_fusion.2 = bf16[256,4096]{1,0:T(8,128)(2,1)} fusion(bf16[768,256]{1,0:T(8,128)(2,1)S(1)} %get-tuple-element.17, bf16[768,4096]{1,0:T(8,128)(2,1)} %all-gather.2.cloned.1.call-done), kind=kOutput, calls=%fused_computation.9 | convolution fusion | flops 1611661312 | bytes 8781824 | tf_op jit(solution)/shard_map/dot_general | solution.py:98
  170.0 1.3 collective-permute-start.3
  171.3 4.3 collective-permute-done.3
  175.7 3.0 add_convert_fusion
  178.7 1.6 copy.49
  180.3 9.8 %fusion.2 = bf16[4096,768]{0,1:T(8,128)(2,1)} fusion(bf16[768,768]{0,1:T(8,128)(2,1)S(1)} %bitcast.131, bf16[768,4096]{0,1:T(8,128)(2,1)} %bitcast.1), kind=kOutput, calls=%fused_computation.8 | convolution fusion | flops 4834983936 | bytes 13762560 | tf_op jit(solution)/shard_map/dot_general | solution.py:147
  191.0 4.4 convolution_convert_fusion
  196.7 9.7 %bitcast_convert_fusion = bf16[768,4096]{1,0:T(8,128)(2,1)} fusion(bf16[768,3,256]{2,0,1:T(8,128)(2,1)S(1)} %copy-done.4, bf16[4096,3,256]{2,0,1:T(8,128)(2,1)} %param.8), kind=kOutput, calls=%fused_computation | convolution fusion | flops 4834983936 | bytes 13762560 | tf_op jit(solution)/shard_map/dot_general | solution.py:140
  207.7 1.3 convolution_bitcast_fusion.1
  209.0 7.5 %rev.6 = f32[16,128,128]{2,1,0:T(8,128)S(1)} reverse(f32[16,128,128]{2,1,0:T(8,128)} %convolution_bitcast_fusion.1), dimensions={2} | reverse | bytes 2097152 | tf_op jit(solution)/shard_map/rev | solution.py:48
  218.0 1.5 slice.177
  219.5 6.3 %reshape.73 = f32[16,128,255]{2,1,0:T(8,128)} reshape(f32[16,32640]{1,0:T(8,128)} %slice.177) | data formatting | bytes 4177920 | tf_op jit(solution)/shard_map/reshape | solution.py:53
  225.8 1.8 reduce_sum.18
  227.6 1.3 convolution_bitcast_fusion
  228.9 7.5 %rev.7 = f32[16,128,128]{2,1,0:T(8,128)S(1)} reverse(f32[16,128,128]{2,1,0:T(8,128)} %convolution_bitcast_fusion), dimensions={2} | reverse | bytes 2097152 | tf_op jit(solution)/shard_map/rev | solution.py:48
  237.9 1.5 slice.179
  239.4 6.2 %reshape.75 = f32[16,128,255]{2,1,0:T(8,128)} reshape(f32[16,32640]{1,0:T(8,128)} %slice.179) | data formatting | bytes 4177920 | tf_op jit(solution)/shard_map/reshape | solution.py:53
  245.6 1.8 reduce_sum.19
  247.5 22.2 %psum.7 = f32[128,16]{0,1:T(8,128)} all-reduce(f32[128,16]{0,1:T(8,128)S(1)} %fusion.35), channel_id=1, replica_groups=mesh['ctx'=8,'tp'=16] {'ctx'}, use_global_device_ids=true, to_apply=%region_6.7 | all-reduce | flops 2048 | bytes 16384 | tf_op jit(solution)/shard_map/psum | solution.py:131
  269.7 1.8 convert_element_type.140
  271.5 14.9 %reduce-scatter.9.cloned.1.call-done = bf16[512,768]{0,1:T(8,128)(2,1)} async-done(((bf16[4096,768]{0,1:T(8,128)(2,1)}), bf16[512,768]{0,1:T(8,128)(2,1)}) %reduce-scatter.9.cloned.1.call-update) | async-done | bytes 786448 | tf_op jit(solution)/shard_map/reduce_scatter | solution.py:146
  286.4 2.5 copy.54
  289.0 90.6 %reduce-scatter.5.cloned.1.call-done = bf16[768,256]{1,0:T(8,128)(2,1)} async-done(((bf16[768,4096]{1,0:T(8,128)(2,1)}), bf16[768,256]{1,0:T(8,128)(2,1)}) %reduce-scatter.5.cloned.1.call-update) | async-done | bytes 393232 | tf_op jit(solution)/shard_map/reduce_scatter | solution.py:91
  379.6 93.8 %reduce-scatter.7.cloned.1.call-done = bf16[768,256]{1,0:T(8,128)(2,1)} async-done(((bf16[768,4096]{1,0:T(8,128)(2,1)}), bf16[768,256]{1,0:T(8,128)(2,1)}) %reduce-scatter.7.cloned.1.call-update) | async-done | bytes 393232 | tf_op jit(solution)/shard_map/reduce_scatter | solution.py:143
  (93 shorter events, 17.5 us)
Async XLA Ops:
  7.2 123.5 %copy-start = (bf16[256,4096]{1,0:T(8,128)(2,1)S(1)}, bf16[256,4096]{1,0:T(8,128)(2,1)}, u32[]{:S(2)}) copy-start(bf16[256,4096]{1,0:T(8,128)(2,1)} %param.9) | copy-start | bytes 6291460
  7.2 123.5 %all-gather.2.cloned.1.call-start = ((), (), s32[]{:S(2)}) async-start(), calls=%async_computation.6 | async-start | bytes 6684672 | tf_op jit(solution)/shard_map/all_gather | solution.py:94
  12.3 86.7 %all-to-all-start = ((bf16[16,768,256]{1,2,0:T(8,128)(2,1)}), bf16[16,768,256]{1,2,0:T(8,128)(2,1)}, u32[]{:S(2)}, u32[]{:S(2)}) async-start(bf16[16,768,256]{1,2,0:T(8,128)(2,1)} %stack.14), calls=%async_computation | async-start | bytes 12582912 | tf_op jit(solution)/shard_map/all_to_all | solution.py:64
  20.5 9.0 %copy-start.21 = (f32[7,3,256]{2,0,1:T(8,128)S(1)}, f32[7,3,256]{2,0,1:T(8,128)}, u32[]{:S(2)}) copy-start(f32[7,3,256]{2,0,1:T(8,128)} %param.10) | copy-start | bytes 64516
  20.5 9.0 %copy-start.23 = (bf16[128,16]{0,1:T(8,128)(2,1)S(1)}, bf16[128,16]{0,1:T(8,128)(2,1)}, u32[]{:S(2)}) copy-start(bf16[128,16]{0,1:T(8,128)(2,1)} %param.12) | copy-start | bytes 12292
  20.5 249.2 %reduce-scatter.11.cloned.1.call-start = ((), (), s32[]{:S(2)}) async-start(), calls=%async_computation.9 | async-start | bytes 2359296 | tf_op jit(solution)/shard_map/reduce_scatter | solution.py:101
  29.5 87.8 %copy-start.15 = (f32[3,256]{1,0:T(4,128)}, f32[3,256]{1,0:T(4,128)S(1)}, u32[]{:S(2)}) copy-start(f32[3,256]{1,0:T(4,128)S(1)} %get-tuple-element.31) | copy-start | bytes 9220
  29.5 87.8 %copy-start.17 = (f32[3,256]{1,0:T(4,128)}, f32[3,256]{1,0:T(4,128)S(1)}, u32[]{:S(2)}) copy-start(f32[3,256]{1,0:T(4,128)S(1)} %get-tuple-element.32) | copy-start | bytes 9220
  108.3 9.0 %collective-permute-start = (bf16[6,3,256]{2,0,1:T(8,128)(2,1)S(1)}, bf16[6,3,256]{2,0,1:T(8,128)(2,1)S(1)}, u32[]{:S(2)}, u32[]{:S(2)}) collective-permute-start(bf16[6,3,256]{2,0,1:T(8,128)(2,1)S(1)} %bitcast.135), channel_id=1, source_target_pairs={{0,16},{16,32},{32,48},{48,64},{64,80},{80,96},{96,112},{1,17},{17... | collective-permute-start | bytes 27656 | tf_op jit(solution)/shard_map/ppermute | solution.py:14
  114.3 3.0 copy-start.19
  119.5 1.4 copy-start.1
  120.9 1.1 copy-start.7
  121.9 1.4 copy-start.11
  136.8 6.3 %copy-start.8 = (bf16[768,256]{1,0:T(8,128)(2,1)}, bf16[768,256]{1,0:T(8,128)(2,1)S(1)}, u32[]{:S(2)}) copy-start(bf16[768,256]{1,0:T(8,128)(2,1)S(1)} %get-tuple-element.19) | copy-start | bytes 1179652
  136.8 10.9 %copy-start.5 = (bf16[768,256]{1,0:T(8,128)(2,1)}, bf16[768,256]{1,0:T(8,128)(2,1)S(1)}, u32[]{:S(2)}) copy-start(bf16[768,256]{1,0:T(8,128)(2,1)S(1)} %get-tuple-element.18) | copy-start | bytes 1179652
  137.0 8.8 %collective-permute-start.2 = (bf16[127,256]{1,0:T(8,128)(2,1)S(1)}, bf16[127,256]{1,0:T(8,128)(2,1)S(1)}, u32[]{:S(2)}, u32[]{:S(2)}) collective-permute-start(bf16[127,256]{1,0:T(8,128)(2,1)S(1)} %slice.169), channel_id=1, source_target_pairs={{16,0},{32,16},{48,32},{64,48},{80,64},{96,80},{112,96},{17,1},{33... | collective-permute-start | bytes 195080 | tf_op jit(solution)/shard_map/ppermute | solution.py:14
  138.3 7.5 %collective-permute-start.1 = (bf16[127,256]{1,0:T(8,128)(2,1)S(1)}, bf16[127,256]{1,0:T(8,128)(2,1)S(1)}, u32[]{:S(2)}, u32[]{:S(2)}) collective-permute-start(bf16[127,256]{1,0:T(8,128)(2,1)S(1)} %slice.168), channel_id=1, source_target_pairs={{0,16},{16,32},{32,48},{48,64},{64,80},{80,96},{96,112},{1,17},{17... | collective-permute-start | bytes 195080 | tf_op jit(solution)/shard_map/ppermute | solution.py:14
  151.9 4.7 copy-start.6
  156.7 2.1 copy-start.9
  158.5 1.6 copy-start.22
  163.1 0.7 copy-start.2
  169.8 116.7 %reduce-scatter.9.cloned.1.call-start = ((), (), s32[]{:S(2)}) async-start(), calls=%async_computation.8 | async-start | bytes 7077888 | tf_op jit(solution)/shard_map/reduce_scatter | solution.py:146
  169.8 5.9 %copy-start.16 = (f32[3,256]{1,0:T(4,128)S(1)}, f32[3,256]{1,0:T(4,128)}, u32[]{:S(2)}) copy-start(f32[3,256]{1,0:T(4,128)} %copy-done.15) | copy-start | bytes 9220
  169.8 5.9 %copy-start.18 = (f32[3,256]{1,0:T(4,128)S(1)}, f32[3,256]{1,0:T(4,128)}, u32[]{:S(2)}) copy-start(f32[3,256]{1,0:T(4,128)} %copy-done.17) | copy-start | bytes 9220
  169.8 5.9 %copy-start.20 = (f32[1,3,256]{2,1,0:T(4,128)S(1)}, f32[1,3,256]{2,1,0:T(4,128)}, u32[]{:S(2)}) copy-start(f32[1,3,256]{2,1,0:T(4,128)} %copy-done.19) | copy-start | bytes 9220
  170.0 5.6 %collective-permute-start.3 = (bf16[6,3,256]{2,0,1:T(8,128)(2,1)S(1)}, bf16[6,3,256]{2,0,1:T(8,128)(2,1)S(1)}, u32[]{:S(2)}, u32[]{:S(2)}) collective-permute-start(bf16[6,3,256]{2,0,1:T(8,128)(2,1)S(1)} %slice.170), channel_id=1, source_target_pairs={{16,0},{32,16},{48,32},{64,48},{80,64},{96,80},{112,96},{17,1},{33... | collective-permute-start | bytes 27656 | tf_op jit(solution)/shard_map/ppermute | solution.py:14
  190.0 1.0 copy-start.3
  190.0 189.6 %reduce-scatter.5.cloned.1.call-start = ((), (), s32[]{:S(2)}) async-start(), calls=%async_computation.5 | async-start | bytes 6684672 | tf_op jit(solution)/shard_map/reduce_scatter | solution.py:91
  195.5 1.3 copy-start.4
  195.5 277.9 %reduce-scatter.7.cloned.1.call-start = ((), (), s32[]{:S(2)}) async-start(), calls=%async_computation.7 | async-start | bytes 6684672 | tf_op jit(solution)/shard_map/reduce_scatter | solution.py:143
  206.5 1.0 copy-start.12
  206.5 1.2 copy-start.13
  219.5 8.1 %copy-start.10 = (bf16[6,128,16,16]{1,0,3,2:T(8,128)(2,1)S(1)}, bf16[6,128,16,16]{1,0,3,2:T(8,128)(2,1)}, u32[]{:S(2)}) copy-start(bf16[6,128,16,16]{1,0,3,2:T(8,128)(2,1)} %copy-done.9) | copy-start | bytes 1179652
  219.5 8.1 %copy-start.14 = (bf16[6,128,16,16]{1,0,3,2:T(8,128)(2,1)S(1)}, bf16[6,128,16,16]{1,0,3,2:T(8,128)(2,1)}, u32[]{:S(2)}) copy-start(bf16[6,128,16,16]{1,0,3,2:T(8,128)(2,1)} %slice.139) | copy-start | bytes 1179652
Sparse Core Ops, SparseCore 0:
  10.4 120.2 all-gather.1
  169.9 41.7 reduce-scatter.10
  214.1 72.3 reduce-scatter.8
  291.0 88.5 reduce-scatter.4
  384.8 88.5 reduce-scatter.6
